TPU v7x, 128 devices: a whole 4x4x4 slice. The times are simulated.
128 devices in a mesh: phrase: 16 (over y, z_lo, core), vocab: 8 (over x, z_hi).
Axes of the slice: x: 4, y: 4, z: 4 (z_hi: 2, z_lo: 2; z = z_hi * 2 + z_lo), core: 2. Of those that a mesh axis runs over, the one named last changes fastest.
Arguments:
- frames: bfloat16 [1536, 1024], P(('phrase', 'vocab'))
- frame_lens: int32 [4], replicated, may hold values from 192 to 384, as said below
- labels: int32 [4, 64], replicated, may hold values from 1 to 4095
- label_lens: int32 [4], replicated, may hold values from 16 to 63, as said below
- phrase_ids: int32 [65536, 8], P(('phrase', 'vocab')), may hold values from 0 to 4095
- phrase_lens: int32 [65536], P(('phrase', 'vocab')), may hold values from 1 to 8
- phrase_table: bfloat16 [4096, 512], replicated, may hold values from -6 to 6
- phrase_w: bfloat16 [512, 512], replicated, may hold values from -0.25 to 0.25
- key_w: bfloat16 [512, 512], replicated, may hold values from -0.25 to 0.25
- value_w: bfloat16 [512, 512], replicated, may hold values from -0.25 to 0.25
- query_w: bfloat16 [1024, 512], replicated, may hold values from -0.9375 to 0.9375
- context_w: bfloat16 [512, 1024], replicated, may hold values from -0.25 to 0.25
- joint_enc_w: bfloat16 [1024, 640], replicated, may hold values from -0.1875 to 0.1875
- pred_table: bfloat16 [4096, 640], replicated, may hold values from -6 to 6
- pred_w: bfloat16 [640, 640], replicated, may hold values from -0.25 to 0.25
- out_w: bfloat16 [640, 4096], P(None, 'vocab')
Outputs:
- blank_logp: float32 [1536, 64], P('phrase', 'vocab')
- label_logp: float32 [1536, 64], P('phrase', 'vocab')
Inputs may be any that keep to these rules, and one draw needn't show every extreme that they name: `frame_lens`: some utterance has exactly 384 frames. `label_lens`: some utterance has exactly 63 labels.
All inputs are finite; a program needn't handle non-finite values.
Results may differ from a plain program's by a relative error of at most 0.0034.
Values may be sent and summed in bfloat16 or wider, within the bound.
No kernel may reach another device: no remote copies, remote signals or barrier semaphores. Data moves between devices by JAX's collectives and lax.ppermute only.
A program may use at most 128 MiB of HBM per device.

v0:
```python
import math
import jax
import jax.numpy as jnp
from jax import lax
from jax.sharding import PartitionSpec as P

HEADS = 4


def encode_local(ids, lens, phrase_table, phrase_w):
    emb = phrase_table[ids]
    mask = (jnp.arange(ids.shape[1], dtype=jnp.int32)[None, :] < lens[:, None]).astype(jnp.bfloat16)
    summed = jnp.einsum("npe,np->ne", emb, mask, preferred_element_type=jnp.float32)
    mean = (summed / lens[:, None].astype(jnp.float32)).astype(jnp.bfloat16)
    return jnp.tanh(jnp.dot(mean, phrase_w, preferred_element_type=jnp.float32)).astype(
        jnp.bfloat16
    )


def block_sums(asked, keys, values, blocks):
    head_size = keys.shape[1] // HEADS
    query_heads = asked.reshape(asked.shape[0], HEADS, head_size)
    key_heads = keys.reshape(keys.shape[0], HEADS, head_size)
    scores = jnp.einsum("fhd,phd->fhp", query_heads, key_heads, preferred_element_type=jnp.float32)
    scores = (scores * (1.0 / math.sqrt(head_size))).reshape(
        asked.shape[0], HEADS, blocks, keys.shape[0] // blocks
    )
    block_peak = jnp.max(scores, -1)
    weights = jnp.exp(scores - block_peak[..., None]).astype(jnp.bfloat16)
    block_total = jnp.sum(weights, -1, dtype=jnp.float32)
    value_heads = values.reshape(blocks, values.shape[0] // blocks, HEADS, head_size)
    block_numer = jnp.einsum(
        "fhbp,bphd->fhbd", weights, value_heads, preferred_element_type=jnp.float32
    )
    return (block_peak, block_total, block_numer)


def rescale(block_peak, block_total, block_numer, peak):
    factor = jnp.exp(block_peak - peak[..., None])
    return (jnp.sum(block_total * factor, -1), jnp.sum(block_numer * factor[..., None], 2))


def local(
    frames,
    frame_lens,
    labels,
    label_lens,
    phrase_ids,
    phrase_lens,
    phrase_table,
    phrase_w,
    key_w,
    value_w,
    query_w,
    context_w,
    joint_enc_w,
    pred_table,
    pred_w,
    out_w,
):
    phrase_vec = encode_local(phrase_ids, phrase_lens, phrase_table, phrase_w)
    keys = jnp.dot(phrase_vec, key_w, preferred_element_type=jnp.float32).astype(jnp.bfloat16)
    values = jnp.dot(phrase_vec, value_w, preferred_element_type=jnp.float32).astype(jnp.bfloat16)
    queries = jnp.dot(frames, query_w, preferred_element_type=jnp.float32).astype(jnp.bfloat16)
    asked = lax.all_gather(queries, ("phrase", "vocab"), axis=0, tiled=True)
    block_peak, block_total, block_numer = block_sums(asked, keys, values, 1)
    peak = lax.pmax(jnp.max(block_peak, -1), ("phrase", "vocab"))
    total, numer = rescale(block_peak, block_total, block_numer, peak)
    total, numer = (
        lax.psum_scatter(total, ("phrase", "vocab"), scatter_dimension=0, tiled=True),
        lax.psum_scatter(numer, ("phrase", "vocab"), scatter_dimension=0, tiled=True),
    )
    context = (numer / total[..., None]).reshape(frames.shape[0], -1).astype(jnp.bfloat16)
    biased = (
        frames.astype(jnp.float32) + jnp.dot(context, context_w, preferred_element_type=jnp.float32)
    ).astype(jnp.bfloat16)
    joint_rows = jnp.dot(biased, joint_enc_w, preferred_element_type=jnp.float32).astype(
        jnp.bfloat16
    )
    joint_all = lax.all_gather(joint_rows, "vocab", axis=0, tiled=True)
    n_vocab = lax.axis_size("vocab")
    vocab_index = lax.axis_index("vocab")
    utts, positions = labels.shape
    own = positions // n_vocab
    width = pred_w.shape[0]
    own_labels = lax.dynamic_slice_in_dim(labels, vocab_index * own, own, 1)
    step_rows = (
        jnp.dot(pred_table[own_labels.reshape(-1)], pred_w, preferred_element_type=jnp.float32)
        .astype(jnp.bfloat16)
        .reshape(utts, own, width)
    )
    step_all = lax.all_gather(step_rows, "vocab", axis=1, tiled=True)
    blank_row = jnp.dot(pred_table[0:1], pred_w, preferred_element_type=jnp.float32).astype(
        jnp.bfloat16
    )
    predictor = jnp.concatenate(
        [jnp.broadcast_to(blank_row[None], (utts, 1, width)), step_all[:, :-1]], 1
    )
    frames_dev = joint_all.shape[0]
    tlen = frames_dev * lax.axis_size("phrase") // utts
    global_index = lax.axis_index("phrase") * frames_dev + jnp.arange(frames_dev, dtype=jnp.int32)
    owner = global_index // tlen
    moment = global_index % tlen
    member = owner[:, None] == jnp.arange(utts, dtype=jnp.int32)[None, :]
    pred_sel = jnp.einsum(
        "fb,buh->fuh", member.astype(jnp.bfloat16), predictor, preferred_element_type=jnp.float32
    )
    joint_in = (
        jnp.tanh(joint_all[:, None, :].astype(jnp.float32) + pred_sel)
        .astype(jnp.bfloat16)
        .reshape(-1, width)
    )
    logits = jnp.dot(joint_in, out_w, preferred_element_type=jnp.float32)
    cols = out_w.shape[1]
    row_labels = jnp.sum(jnp.where(member[:, :, None], labels[None, :, :], 0), 1)
    column = vocab_index * cols + jnp.arange(cols, dtype=jnp.int32)
    label_part = jnp.sum(
        jnp.where(column[None, :] == row_labels.reshape(-1, 1), logits, 0.0), -1
    ).reshape(frames_dev, positions)
    blank_part = jnp.where(vocab_index == 0, logits[:, 0], 0.0).reshape(frames_dev, positions)
    start_own = vocab_index * own
    peak_rows = lax.pmax(jnp.max(logits, -1), "vocab")
    total_part = jnp.sum(jnp.exp(logits - peak_rows[:, None]), -1).reshape(frames_dev, positions)
    peak_own = lax.dynamic_slice_in_dim(peak_rows.reshape(frames_dev, positions), start_own, own, 1)
    total_every = lax.psum(total_part, "vocab")
    total_own = lax.dynamic_slice_in_dim(total_every, start_own, own, 1)
    blank_own, label_own = (
        lax.psum_scatter(blank_part, "vocab", scatter_dimension=1, tiled=True),
        lax.psum_scatter(label_part, "vocab", scatter_dimension=1, tiled=True),
    )
    norm = peak_own + jnp.log(total_own)
    positions_own = start_own + jnp.arange(own, dtype=jnp.int32)
    frame_len = jnp.sum(jnp.where(member, frame_lens[None, :], 0), 1)
    label_len = jnp.sum(jnp.where(member, label_lens[None, :], 0), 1)
    live = (moment < frame_len)[:, None]
    blank_out = jnp.where(
        live & (positions_own[None, :] <= label_len[:, None]), blank_own - norm, 0.0
    )
    label_out = jnp.where(
        live & (positions_own[None, :] < label_len[:, None]), label_own - norm, 0.0
    )
    return (blank_out, label_out)


def solution(mesh):
    in_specs = (
        P(("phrase", "vocab"), None),
        P(),
        P(),
        P(),
        P(("phrase", "vocab"), None),
        P(("phrase", "vocab")),
        P(),
        P(),
        P(),
        P(),
        P(),
        P(),
        P(),
        P(),
        P(),
        P(None, "vocab"),
    )
    out_specs = (P("phrase", "vocab"), P("phrase", "vocab"))
    return jax.shard_map(local, mesh=mesh, in_specs=in_specs, out_specs=out_specs, check_vma=False)
```

profile of v0, /device:TPU:0, one launch (start us, length us, event | category | flops | bytes accessed | tf_op | source)
XLA Modules:
  0.0 752.5 jit_solution(592532760997151571)
XLA Ops:
  7.2 2.2 fusion.14
  12.0 20.2 %gather_fusion = bf16[4096,512]{1,0:T(8,128)(2,1)} fusion(bf16[4096,512]{1,0:T(8,128)(2,1)} %param.22, s32[4096]{0:T(1024)S(1)} %broadcast_clamp_fusion), kind=kCustom, calls=%fused_computation | custom fusion | bytes 8404992 | tf_op jit(solution)/shard_map/gather | solution.py:11
  32.4 3.5 fusion.2
  36.9 1.3 convolution_convert_fusion.1
  38.2 274.2 %all-gather.4.cloned.1.call-done = bf16[128,12,512]{2,1,0:T(8,128)(2,1)} async-done(((bf16[1,12,512]{2,1,0:T(8,128)(2,1)}), bf16[128,12,512]{2,1,0:T(8,128)(2,1)}) %all-gather.4.cloned.1.call-update) | async-done | bytes 1572880 | tf_op jit(solution)/shard_map/all_gather | solution.py:65
  312.4 3.2 reshape.171
  315.6 6.4 bitcast_reduce_fusion
  322.1 66.9 %pmax.14 = f32[1536,4]{0,1:T(4,128)S(1)} all-reduce(f32[1536,4]{0,1:T(4,128)S(1)} %get-tuple-element.19), channel_id=1, replica_groups=mesh['phrase'=16,'vocab'=8] {'phrase','vocab'}, use_global_device_ids=true, to_apply=%region_3.0 | all-reduce | flops 6144 | bytes 49152 | tf_op jit(solution)/shard_map/pmax | solution.py:67
  389.0 6.8 convert_reduce_fusion
  397.2 5.0 fusion.5
  402.2 5.0 copy.48
  407.5 3.8 gather_fusion.1
  411.6 35.0 %all_gather.11 = bf16[4,64,640]{2,0,1:T(4,128)(2,1)S(1)} all-gather(bf16[4,8,640]{2,0,1:T(4,128)(2,1)S(1)} %copy.50), channel_id=1, replica_groups=mesh['phrase'=16,'vocab'=8] {'vocab'}, dimensions={1}, use_global_device_ids=true | all-gather | bytes 368640 | tf_op jit(solution)/shard_map/all_gather | solution.py:92
  449.5 1.2 dynamic-slice.2
  453.1 63.0 %all-reduce.1 = f32[1536,4]{0,1:T(4,128)S(1)} all-reduce(f32[1536,4]{0,1:T(4,128)} %get-tuple-element.15), channel_id=3, replica_groups=mesh['phrase'=16,'vocab'=8] {'phrase','vocab'}, use_global_device_ids=true, to_apply=%region_6.0.clone | all-reduce | flops 6144 | bytes 49152
  516.3 42.6 %all-reduce.8.cloned.1.call-done = f32[1536,4,128]{2,1,0:T(4,128)} async-done(((f32[1536,4,128]{2,1,0:T(4,128)}), f32[1536,4,128]{2,1,0:T(4,128)}) %all-reduce.8.cloned.1.call-update) | async-done | bytes 3145744
  559.8 1.2 fusion.13
  561.0 34.2 %all-gather.1 = bf16[8,12,640]{2,1,0:T(8,128)(2,1)S(1)} all-gather(bf16[1,12,640]{2,1,0:T(8,128)(2,1)S(1)} %fusion.13), channel_id=1, replica_groups=mesh['phrase'=16,'vocab'=8] {'vocab'}, dimensions={0}, use_global_device_ids=true | all-gather | bytes 138240 | tf_op jit(solution)/shard_map/all_gather | solution.py:80
  595.3 3.6 tanh_convert_fusion
  598.9 6.0 copy.51
  605.0 11.2 %fusion.38 = (f32[6144]{0:T(1024)S(1)}, f32[6144,512]{0,1:T(8,128)}) fusion(bf16[6144,640]{1,0:T(8,128)(2,1)} %bitcast.74, bf16[640,512]{1,0:T(8,128)(2,1)S(1)} %copy-done.11), kind=kOutput, calls=%fused_computation.75 | convolution fusion | flops 4029671424 | bytes 21127168 | tf_op jit(solution)/shard_map/dot_general | solution.py:113
  616.2 40.3 %pmax.15 = f32[6144]{0:T(1024)S(1)} all-reduce(f32[6144]{0:T(1024)S(1)} %get-tuple-element.21), channel_id=1, replica_groups=mesh['phrase'=16,'vocab'=8] {'vocab'}, use_global_device_ids=true, to_apply=%region_9.10 | all-reduce | flops 6144 | bytes 49152 | tf_op jit(solution)/shard_map/pmax | solution.py:122
  656.6 6.5 select_reduce_fusion
  666.3 77.4 %all-reduce.10.cloned.1.call-done = (f32[96,64]{1,0:T(8,128)}, f32[96,64]{1,0:T(8,128)}, f32[96,64]{1,0:T(8,128)}) async-done(((f32[96,64]{1,0:T(8,128)}, f32[96,64]{1,0:T(8,128)}, f32[96,64]{1,0:T(8,128)}), (f32[96,64]{1,0:T(8,128)}, f32[96,64]{1,0:T(8,128)}, f32[96,64]{1,0:T(8,128)})) %all-reduce.10.cloned.1.call-update) | async-done | bytes 73744
  (73 shorter events, 16.7 us)
Async XLA Ops:
  7.2 552.6 %copy-start = (bf16[1024,640]{1,0:T(8,128)(2,1)S(1)}, bf16[1024,640]{1,0:T(8,128)(2,1)}, u32[]{:S(2)}) copy-start(bf16[1024,640]{1,0:T(8,128)(2,1)} %param.28) | copy-start | bytes 3932164
  7.2 305.3 %all-gather.4.cloned.1.call-start = ((), (), s32[]{:S(2)}) async-start(), calls=%async_computation | async-start | bytes 2113536 | tf_op jit(solution)/shard_map/all_gather | solution.py:65
  9.4 549.5 %all-reduce.8.cloned.1.call-start = ((), (), s32[]{:S(2)}) async-start(), calls=%async_computation.1 | async-start | bytes 6291456
  12.0 20.2 %copy-start.7 = (s32[512]{0:T(512)S(1)}, s32[512]{0:T(512)}, u32[]{:S(2)}) copy-start(s32[512]{0:T(512)} %param.21) | copy-start | bytes 6148
  12.0 23.9 %copy-start.12 = (bf16[512,512]{1,0:T(8,128)(2,1)S(1)}, bf16[512,512]{1,0:T(8,128)(2,1)}, u32[]{:S(2)}) copy-start(bf16[512,512]{1,0:T(8,128)(2,1)} %param.23) | copy-start | bytes 1572868
  32.2 4.2 copy-start.4
  32.2 4.7 copy-start.5
  389.0 8.2 %copy-start.1 = (f32[4,512,1536]{2,1,0:T(8,128)S(1)}, f32[4,512,1536]{2,1,0:T(8,128)}, u32[]{:S(2)}) copy-start(f32[4,512,1536]{2,1,0:T(8,128)} %get-tuple-element.20) | copy-start | bytes 37748740
  402.2 9.1 %copy-start.2 = (bf16[640,640]{1,0:T(8,128)(2,1)S(1)}, bf16[640,640]{1,0:T(8,128)(2,1)}, u32[]{:S(2)}) copy-start(bf16[640,640]{1,0:T(8,128)(2,1)} %param.30) | copy-start | bytes 2457604
  402.2 45.1 %copy-start.8 = (s32[4,64]{1,0:T(4,128)S(1)}, s32[4,64]{1,0:T(4,128)}, u32[]{:S(2)}) copy-start(s32[4,64]{1,0:T(4,128)} %param.18) | copy-start | bytes 3076
  402.2 49.2 %copy-start.9 = (s32[4]{0:T(128)S(1)}, s32[4]{0:T(128)}, u32[]{:S(2)}) copy-start(s32[4]{0:T(128)} %param.17) | copy-start | bytes 52
  402.2 157.6 %copy-start.3 = (bf16[512,1024]{1,0:T(8,128)(2,1)S(1)}, bf16[512,1024]{1,0:T(8,128)(2,1)}, u32[]{:S(2)}) copy-start(bf16[512,1024]{1,0:T(8,128)(2,1)} %param.27) | copy-start | bytes 3145732
  407.2 336.4 %all-reduce.10.cloned.1.call-start = ((), (), s32[]{:S(2)}) async-start(), calls=%async_computation.2 | async-start | bytes 294912
  446.8 0.5 copy-start.10
  598.9 6.0 copy-start.11
  605.0 51.6 %copy-start.6 = (s32[6144]{0:T(1024)S(1)}, s32[6144]{0:T(1024)}, u32[]{:S(2)}) copy-start(s32[6144]{0:T(1024)} %eq.42) | copy-start | bytes 73732
Sparse Core Ops, SparseCore 0:
  9.7 302.6 all-gather.3
  407.4 151.5 all-reduce.7
  666.3 77.2 all-reduce.9
where the time goes:
time: 753 us
  waiting for transfers between devices  394 us (52%)
  blocking collectives  240 us (32%)
  local copies, waits for them, and re-layouts  47.1 us (6%)
  matrix products  36.7 us (5%)
  other arithmetic  19.8 us (3%)
  between operations  14.7 us (2%)
    all_gather x1, waiting for transfers between devices, local(): asked = lax.all_gather(queries, ('phrase', 'vocab'), axis=0, tiled=True)  274 us
    unnamed x5, waiting for transfers between devices  120 us
    pmax x1, blocking collectives, local(): peak = lax.pmax(jnp.max(block_peak, -1), ('phrase', 'vocab'))  66.9 us
    unnamed x1, blocking collectives  63 us
    pmax x1, blocking collectives, local(): peak_rows = lax.pmax(jnp.max(logits, -1), 'vocab')  40.3 us
    all_gather x1, blocking collectives, local(): step_all = lax.all_gather(step_rows, 'vocab', axis=1, tiled=True)  35 us
    all_gather x1, blocking collectives, local(): joint_all = lax.all_gather(joint_rows, 'vocab', axis=0, tiled=True)  34.2 us
    gather x1, local copies, waits for them, and re-layouts, encode_local(): emb = phrase_table[ids]  20.2 us
  transfers between devices with their start and end apart: 3, of which 3 were waited for; matrix products, arithmetic and copies ran while one was open for 5% of the time, Pallas kernels for 0%

commit v1 on v0

--- a/solution.py
+++ b/solution.py
@@ -5,6 +5,13 @@
 from jax.sharding import PartitionSpec as P
 
 HEADS = 4
+
+
+def gather_over(array, name, dim):
+    size = lax.axis_size(name)
+    blocks = jnp.stack([array for _ in range(size)])
+    blocks = lax.all_to_all(blocks, name, split_axis=0, concat_axis=0)
+    return jnp.concatenate(blocks, axis=dim)
 
 
 def encode_local(ids, lens, phrase_table, phrase_w):
@@ -62,7 +69,7 @@
     keys = jnp.dot(phrase_vec, key_w, preferred_element_type=jnp.float32).astype(jnp.bfloat16)
     values = jnp.dot(phrase_vec, value_w, preferred_element_type=jnp.float32).astype(jnp.bfloat16)
     queries = jnp.dot(frames, query_w, preferred_element_type=jnp.float32).astype(jnp.bfloat16)
-    asked = lax.all_gather(queries, ("phrase", "vocab"), axis=0, tiled=True)
+    asked = gather_over(queries, ("phrase", "vocab"), 0)
     block_peak, block_total, block_numer = block_sums(asked, keys, values, 1)
     peak = lax.pmax(jnp.max(block_peak, -1), ("phrase", "vocab"))
     total, numer = rescale(block_peak, block_total, block_numer, peak)

time: 753 us -> 491 us (0.65)
  waiting for transfers between devices: 394 us -> 122 us
  starting transfers between devices: 0.3 us -> 11.8 us
    all_gather x1 -> x0, waiting for transfers between devices: 274 us -> none  [local(): asked = lax.all_gather(queries, ('phrase', 'vocab'), axis=0, tiled=True)]
    all_to_all x0 -> x1, starting transfers between devices: none -> 11.7 us  [gather_over(): blocks = lax.all_to_all(blocks, name, split_axis=0, concat_axis=0)]
    unnamed x5 -> x4, waiting for transfers between devices: 120 us -> 121 us
  transfers between devices with their start and end apart: 3 -> 3, of which waited for: 3 -> 3; matrix products, arithmetic and copies ran while one was open for 5% -> 8% of each run, Pallas kernels for 0% -> 0%
where the time goes in v1:
time: 491 us; the launch traced here: 490 us
  blocking collectives  238 us (48%)
  waiting for transfers between devices  122 us (25%)
  local copies, waits for them, and re-layouts  48.1 us (10%)
  matrix products  36.1 us (7%)
  other arithmetic  19.1 us (4%)
  between operations  15.1 us (3%)
  starting transfers between devices  11.8 us (2%)
    unnamed x4, waiting for transfers between devices  121 us
    pmax x1, blocking collectives, local(): peak = lax.pmax(jnp.max(block_peak, -1), ('phrase', 'vocab'))  66.1 us
    unnamed x1, blocking collectives  62.9 us
    pmax x1, blocking collectives, local(): peak_rows = lax.pmax(jnp.max(logits, -1), 'vocab')  40.3 us
    all_gather x1, blocking collectives, local(): step_all = lax.all_gather(step_rows, 'vocab', axis=1, tiled=True)  34.7 us
    all_gather x1, blocking collectives, local(): joint_all = lax.all_gather(joint_rows, 'vocab', axis=0, tiled=True)  34.5 us
    gather x1, local copies, waits for them, and re-layouts, encode_local(): emb = phrase_table[ids]  20.2 us
    all_to_all x1, starting transfers between devices, gather_over(): blocks = lax.all_to_all(blocks, name, split_axis=0, concat_axis=0)  11.7 us
  transfers between devices with their start and end apart: 3, of which 3 were waited for; matrix products, arithmetic and copies ran while one was open for 8% of the time, Pallas kernels for 0%

profile of v1, /device:TPU:0, one launch (start us, length us, event | category | flops | bytes accessed | tf_op | source)
XLA Modules:
  0.0 490.4 jit_solution(4134264136174751395)
XLA Ops:
  7.2 1.6 convolution_convert_fusion.3
  8.8 1.6 stack.2
  10.4 11.7 %all-to-all-start = ((bf16[128,12,512]{2,1,0:T(8,128)(2,1)}), bf16[128,12,512]{2,1,0:T(8,128)(2,1)}, u32[]{:S(2)}, u32[]{:S(2)}) async-start(bf16[128,12,512]{2,1,0:T(8,128)(2,1)} %stack.2), calls=%async_computation | async-start | bytes 4194304 | tf_op jit(solution)/shard_map/all_to_all | solution.py:13
  23.4 20.2 %gather_fusion = bf16[4096,512]{1,0:T(8,128)(2,1)} fusion(bf16[4096,512]{1,0:T(8,128)(2,1)} %param.22, s32[4096]{0:T(1024)S(1)} %broadcast_clamp_fusion), kind=kCustom, calls=%fused_computation | custom fusion | bytes 8404992 | tf_op jit(solution)/shard_map/gather | solution.py:18
  43.7 3.5 fusion.2
  48.2 1.3 convolution_convert_fusion.1
  50.7 3.2 reshape_reshape.3
  53.9 6.4 %bitcast_reduce_fusion = (f32[1536,4]{0,1:T(4,128)S(1)}, f32[4,512,1536]{2,1,0:T(8,128)}) fusion(bf16[512,4,128]{0,2,1:T(8,128)(2,1)S(1)} %bitcast.73, bf16[1536,4,128]{2,1,0:T(4,128)(2,1)S(1)} %reshape_reshape.3), kind=kOutput, calls=%fused_computation.4 | convolution fusion | flops 811591680 | bytes 14704640 | tf_op jit(solution)/shard_map/fhd,phd->fhp/dot_general | solution.py:31
  60.4 66.1 %pmax.14 = f32[1536,4]{0,1:T(4,128)S(1)} all-reduce(f32[1536,4]{0,1:T(4,128)S(1)} %get-tuple-element.19), channel_id=1, replica_groups=mesh['phrase'=16,'vocab'=8] {'phrase','vocab'}, use_global_device_ids=true, to_apply=%region_3.0 | all-reduce | flops 6144 | bytes 49152 | tf_op jit(solution)/shard_map/pmax | solution.py:74
  126.5 6.8 %convert_reduce_fusion = f32[1536,4]{0,1:T(4,128)S(1)} fusion(f32[1536,4]{0,1:T(4,128)S(1)} %get-tuple-element.19, f32[4,512,1536]{2,1,0:T(8,128)} %get-tuple-element.20), kind=kLoop, calls=%fused_computation.9 | loop fusion | flops 15722496 | bytes 12632064 | tf_op jit(solution)/shard_map/reduce_sum | solution.py:37
  134.6 5.0 %fusion.5 = f32[1536,4,128]{0,2,1:T(8,128)} fusion(bf16[512,4,128]{0,2,1:T(8,128)(2,1)} %bitcast.74, f32[1536,4]{0,1:T(4,128)S(1)} %get-tuple-element.16, f32[4,512,1536]{2,1,0:T(8,128)S(1)} %copy-done.1, f32[1536,4]{0,1:T(4,128)S(1)} %get-tuple-element.19), kind=kOutput, calls=%fused_computation.14 | convolution fusion | flops 815529984 | bytes 16302080 | tf_op jit(solution)/shard_map/fhbp,bphd->fhbd/dot_general | solution.py:39
  139.7 5.0 %copy.47 = f32[1536,4,128]{2,1,0:T(4,128)} copy(f32[1536,4,128]{0,2,1:T(8,128)} %fusion.5) | data formatting | bytes 6291456 | tf_op jit(solution)/shard_map/reduce_sum | solution.py:47
  144.8 3.8 gather_fusion.1
  148.9 34.7 %all_gather.7 = bf16[4,64,640]{2,0,1:T(4,128)(2,1)S(1)} all-gather(bf16[4,8,640]{2,0,1:T(4,128)(2,1)S(1)} %copy.49), channel_id=1, replica_groups=mesh['phrase'=16,'vocab'=8] {'vocab'}, dimensions={1}, use_global_device_ids=true | all-gather | bytes 368640 | tf_op jit(solution)/shard_map/all_gather | solution.py:99
  186.5 1.2 dynamic-slice.2
  190.1 62.9 %all-reduce.1 = f32[1536,4]{0,1:T(4,128)S(1)} all-reduce(f32[1536,4]{0,1:T(4,128)} %get-tuple-element.15), channel_id=3, replica_groups=mesh['phrase'=16,'vocab'=8] {'phrase','vocab'}, use_global_device_ids=true, to_apply=%region_6.0.clone | all-reduce | flops 6144 | bytes 49152
  253.2 43.2 %all-reduce.8.cloned.1.call-done = f32[1536,4,128]{2,1,0:T(4,128)} async-done(((f32[1536,4,128]{2,1,0:T(4,128)}), f32[1536,4,128]{2,1,0:T(4,128)}) %all-reduce.8.cloned.1.call-update) | async-done | bytes 3145744
  298.4 34.5 %all-gather = bf16[8,12,640]{2,1,0:T(8,128)(2,1)S(1)} all-gather(bf16[1,12,640]{2,1,0:T(8,128)(2,1)S(1)} %fusion.13), channel_id=1, replica_groups=mesh['phrase'=16,'vocab'=8] {'vocab'}, dimensions={0}, use_global_device_ids=true | all-gather | bytes 138240 | tf_op jit(solution)/shard_map/all_gather | solution.py:87
  332.9 3.6 tanh_convert_fusion
  336.5 6.0 %copy.50 = bf16[96,64,640]{2,1,0:T(8,128)(2,1)} copy(bf16[96,64,640]{2,0,1:T(8,128)(2,1)S(1)} %tanh_convert_fusion) | data formatting | bytes 15728640 | tf_op jit(solution)/shard_map/convert_element_type | solution.py:117
  342.6 11.2 %fusion.37 = (f32[6144]{0:T(1024)S(1)}, f32[6144,512]{0,1:T(8,128)}) fusion(bf16[6144,640]{1,0:T(8,128)(2,1)} %bitcast.72, bf16[640,512]{1,0:T(8,128)(2,1)S(1)} %copy-done.11), kind=kOutput, calls=%fused_computation.74 | convolution fusion | flops 4029671424 | bytes 21127168 | tf_op jit(solution)/shard_map/dot_general | solution.py:120
  353.8 40.3 %pmax.15 = f32[6144]{0:T(1024)S(1)} all-reduce(f32[6144]{0:T(1024)S(1)} %get-tuple-element.21), channel_id=1, replica_groups=mesh['phrase'=16,'vocab'=8] {'vocab'}, use_global_device_ids=true, to_apply=%region_9.10 | all-reduce | flops 6144 | bytes 49152 | tf_op jit(solution)/shard_map/pmax | solution.py:129
  394.2 6.5 %select_reduce_fusion = (f32[6144]{0:T(1024)S(1)}, f32[6144]{0:T(1024)S(1)}) fusion(f32[6144,512]{0,1:T(8,128)} %get-tuple-element.22, s32[6144]{0:T(1024)S(1)} %copy-done.6, s32[512]{0:T(512)S(1)} %iota_add_fusion, f32[6144]{0:T(1024)S(1)} %pmax.15), kind=kLoop, calls=%fused_computation.7 | loop fusion | flops 15716352 | bytes 12683264 | tf_op jit(solution)/shard_map/reduce_sum | solution.py:124
  403.9 77.4 %all-reduce.10.cloned.1.call-done = (f32[96,64]{1,0:T(8,128)}, f32[96,64]{1,0:T(8,128)}, f32[96,64]{1,0:T(8,128)}) async-done(((f32[96,64]{1,0:T(8,128)}, f32[96,64]{1,0:T(8,128)}, f32[96,64]{1,0:T(8,128)}), (f32[96,64]{1,0:T(8,128)}, f32[96,64]{1,0:T(8,128)}, f32[96,64]{1,0:T(8,128)})) %all-reduce.10.cloned.1.call-update) | async-done | bytes 73744
  (73 shorter events, 17.5 us)
Async XLA Ops:
  7.2 290.0 %copy-start = (bf16[1024,640]{1,0:T(8,128)(2,1)S(1)}, bf16[1024,640]{1,0:T(8,128)(2,1)}, u32[]{:S(2)}) copy-start(bf16[1024,640]{1,0:T(8,128)(2,1)} %param.28) | copy-start | bytes 3932164
  7.2 16.0 %copy-start.7 = (s32[512]{0:T(512)S(1)}, s32[512]{0:T(512)}, u32[]{:S(2)}) copy-start(s32[512]{0:T(512)} %param.21) | copy-start | bytes 6148
  7.2 16.0 %copy-start.8 = (s32[4,64]{1,0:T(4,128)S(1)}, s32[4,64]{1,0:T(4,128)}, u32[]{:S(2)}) copy-start(s32[4,64]{1,0:T(4,128)} %param.18) | copy-start | bytes 3076
  10.4 40.3 %all-to-all-start = ((bf16[128,12,512]{2,1,0:T(8,128)(2,1)}), bf16[128,12,512]{2,1,0:T(8,128)(2,1)}, u32[]{:S(2)}, u32[]{:S(2)}) async-start(bf16[128,12,512]{2,1,0:T(8,128)(2,1)} %stack.2), calls=%async_computation | async-start | bytes 4194304 | tf_op jit(solution)/shard_map/all_to_all | solution.py:13
  22.1 274.2 %all-reduce.8.cloned.1.call-start = ((), (), s32[]{:S(2)}) async-start(), calls=%async_computation.1 | async-start | bytes 6291456
  23.4 23.8 %copy-start.12 = (bf16[512,512]{1,0:T(8,128)(2,1)S(1)}, bf16[512,512]{1,0:T(8,128)(2,1)}, u32[]{:S(2)}) copy-start(bf16[512,512]{1,0:T(8,128)(2,1)} %param.23) | copy-start | bytes 1572868
  43.5 4.2 copy-start.4
  43.5 4.7 copy-start.5
  126.5 8.2 %copy-start.1 = (f32[4,512,1536]{2,1,0:T(8,128)S(1)}, f32[4,512,1536]{2,1,0:T(8,128)}, u32[]{:S(2)}) copy-start(f32[4,512,1536]{2,1,0:T(8,128)} %get-tuple-element.20) | copy-start | bytes 37748740
  139.7 8.9 %copy-start.2 = (bf16[640,640]{1,0:T(8,128)(2,1)S(1)}, bf16[640,640]{1,0:T(8,128)(2,1)}, u32[]{:S(2)}) copy-start(bf16[640,640]{1,0:T(8,128)(2,1)} %param.30) | copy-start | bytes 2457604
  139.7 48.7 %copy-start.9 = (s32[4]{0:T(128)S(1)}, s32[4]{0:T(128)}, u32[]{:S(2)}) copy-start(s32[4]{0:T(128)} %param.17) | copy-start | bytes 52
  139.7 157.5 %copy-start.3 = (bf16[512,1024]{1,0:T(8,128)(2,1)S(1)}, bf16[512,1024]{1,0:T(8,128)(2,1)}, u32[]{:S(2)}) copy-start(bf16[512,1024]{1,0:T(8,128)(2,1)} %param.27) | copy-start | bytes 3145732
  144.7 336.6 %all-reduce.10.cloned.1.call-start = ((), (), s32[]{:S(2)}) async-start(), calls=%async_computation.2 | async-start | bytes 294912
  183.7 0.5 copy-start.10
  336.5 6.0 %copy-start.11 = (bf16[640,512]{1,0:T(8,128)(2,1)S(1)}, bf16[640,512]{1,0:T(8,128)(2,1)}, u32[]{:S(2)}) copy-start(bf16[640,512]{1,0:T(8,128)(2,1)} %param.31) | copy-start | bytes 1966084
  342.6 51.6 %copy-start.6 = (s32[6144]{0:T(1024)S(1)}, s32[6144]{0:T(1024)}, u32[]{:S(2)}) copy-start(s32[6144]{0:T(1024)} %eq.42) | copy-start | bytes 73732
Sparse Core Ops, SparseCore 0:
  144.8 151.4 all-reduce.7
  403.9 77.2 all-reduce.9
